TPU v7x, 32 devices: a whole 2x2x4 slice. The times are simulated.
32 devices in a mesh: dp: 16 (over z, x, core), mp: 2 (over y).
Axes of the slice: x: 2, y: 2, z: 4, core: 2. Of those that a mesh axis runs over, the one named last changes fastest.
Arguments:
- inputs: bfloat16 [8192, 3968], P('dp', 'mp'), may hold values from -6 to 6
- grad_out: bfloat16 [8192, 2048], P('dp', 'mp'), may hold values from -0.25 to 0.25
- error: bfloat16 [32768, 3968], P(('dp', 'mp')), may hold values from -6 to 6
- q_prev: float32 [3968, 64], P('mp'), may hold values from -0.09375 to 0.09375
Outputs:
- new_error: bfloat16 [32768, 3968], P(('dp', 'mp'))
- p_basis: float32 [2048, 64], P('mp')
- q_factor: float32 [3968, 64], P('mp')
All inputs are finite; a program needn't handle non-finite values.
Results may differ from a plain program's by a relative error of at most 0.0065.
Values may be sent and summed in bfloat16 or wider, within the bound.
A program may use at most 64 MiB of HBM per device.

v0:
```python
import jax
import jax.numpy as jnp
from jax import lax
from jax.sharding import PartitionSpec as P


def per_device(inputs, grad_out, error, q_prev):
    highest = lax.Precision.HIGHEST
    replicas = lax.axis_size("dp")
    shards = lax.axis_size("mp")
    own_rows = grad_out.shape[1]
    rank = q_prev.shape[1]
    q_full = lax.all_gather(q_prev, "mp", axis=0, tiled=True)
    prod = lax.dot_general(
        grad_out,
        lax.all_gather(inputs, "mp", axis=1, tiled=True),
        (((0,), (0,)), ((), ())),
        preferred_element_type=jnp.float32,
    )
    merged = prod + error.astype(jnp.float32)
    local_p = jnp.dot(merged, q_full, precision=highest)
    factor = lax.psum(local_p, "dp") / replicas
    gram = lax.psum(jnp.dot(factor.T, factor, precision=highest), "mp")
    ridge = 0.01 * jnp.trace(gram) / rank + 1e-06
    gram = gram + ridge * jnp.eye(rank, dtype=jnp.float32)
    lower = jnp.linalg.cholesky(gram)
    p_hat = jax.scipy.linalg.solve_triangular(lower, factor.T, lower=True).T
    q_term = lax.dot_general(merged, p_hat, (((0,), (0,)), ((), ())), precision=highest)
    q_part = lax.psum_scatter(
        q_term.astype(jnp.bfloat16), "mp", scatter_dimension=0, tiled=True
    ).astype(jnp.float32)
    q_own = lax.psum(q_part, "dp") / replicas
    q_whole = lax.all_gather(q_own.astype(jnp.bfloat16), "mp", axis=0, tiled=True).astype(
        q_own.dtype
    )
    approx = jnp.dot(p_hat, q_whole.T, precision=highest)
    new_error = (merged - approx).astype(jnp.bfloat16)
    scale = jnp.sqrt(jnp.float32(own_rows * shards))
    return (new_error, p_hat * scale, q_own)


def solution(mesh):
    return jax.shard_map(
        per_device,
        mesh=mesh,
        in_specs=(P("dp", "mp"), P("dp", "mp"), P(("dp", "mp"), None), P("mp", None)),
        out_specs=(P(("dp", "mp"), None), P("mp", None), P("mp", None)),
        check_vma=False,
    )
```

profile of v0, /device:TPU:0, one launch (start us, length us, event | category | flops | bytes accessed | tf_op | source)
XLA Modules:
  0.0 344.3 jit_solution(4589532724388104578)
XLA Ops:
  7.2 0.7 all-gather.4.cloned.1.call-update
  8.0 17.7 %all-gather = f32[2,1984,64]{1,2,0:T(8,128)S(1)} all-gather(f32[1,1984,64]{1,2,0:T(8,128)} %bitcast.27), channel_id=1, replica_groups=mesh['dp'=16,'mp'=2] {'mp'}, dimensions={0}, use_global_device_ids=true | all-gather | bytes 1523712 | tf_op jit(solution)/shard_map/all_gather | solution.py:13
  25.7 0.8 copy.11
  26.5 1.1 reshape.17
  27.6 40.0 %all-gather.4.cloned.1.call-done = bf16[512,3968]{0,1:T(8,128)(2,1)} async-done(((bf16[512,1984]{0,1:T(8,128)(2,1)}), bf16[512,3968]{0,1:T(8,128)(2,1)}) %all-gather.4.cloned.1.call-update) | async-done | bytes 4063248 | tf_op jit(solution)/shard_map/all_gather | solution.py:16
  67.6 8.4 %convert_add_fusion = f32[1024,3968]{1,0:T(8,128)S(1)} fusion(bf16[1024,3968]{1,0:T(8,128)(2,1)} %param.6, bf16[512,1024]{1,0:T(8,128)(2,1)S(1)} %copy-done, bf16[512,3968]{0,1:T(8,128)(2,1)} %all-gather.4.cloned.1.call-done), kind=kOutput, calls=%fused_computation.1 | convolution fusion | flops 4168876032 | bytes 29491200 | tf_op jit(solution)/shard_map/dot_general | solution.py:14
  76.0 5.6 %copy-done.1 = f32[1024,3968]{1,0:T(8,128)} copy-done((f32[1024,3968]{1,0:T(8,128)}, f32[1024,3968]{1,0:T(8,128)S(1)}, u32[]{:S(2)}) %copy-start.1) | copy-done | bytes 16252952
  81.7 16.6 %fusion.11 = f32[1024,64]{0,1:T(8,128)} fusion(f32[1024,3968]{1,0:T(8,128)S(1)} %convert_add_fusion, f32[3968,64]{0,1:T(8,128)S(1)} %reshape.17), kind=kOutput, calls=%fused_computation.25 | convolution fusion | flops 3120562176 | bytes 17530880 | tf_op jit(solution)/shard_map/dot_general | solution.py:21
  98.6 91.1 %all-reduce.3.cloned.1.call-done = f32[1024,64]{0,1:T(8,128)} async-done(((f32[1024,64]{0,1:T(8,128)}), f32[1024,64]{0,1:T(8,128)}) %all-reduce.3.cloned.1.call-update) | async-done | bytes 262160 | tf_op jit(solution)/shard_map/psum | solution.py:22
  189.7 1.4 fusion.2
  191.1 8.3 %psum.22 = f32[64,64]{1,0:T(8,128)S(1)} all-reduce(f32[64,64]{1,0:T(8,128)S(1)} %fusion.2), channel_id=1, replica_groups=mesh['dp'=16,'mp'=2] {'mp'}, use_global_device_ids=true, to_apply=%region_1.0 | all-reduce | flops 4096 | bytes 32768 | tf_op jit(solution)/shard_map/psum | solution.py:23
  200.8 5.8 %cholesky.17 = f32[64,64]{1,0:T(8,128)S(1)} custom-call(f32[64,64]{1,0:T(8,128)S(1)} %fusion.8), custom_call_target="Cholesky" | custom-call | tf_op jit(solution)/shard_map/jit(cholesky)/cholesky | solution.py:26
  207.3 0.7 fusion.6
  208.0 4.9 %custom-call.7 = f32[1,64,64]{1,2,0:T(8,128)S(1)} custom-call(f32[1,64,64]{2,1,0:T(8,128)S(1)} %fusion.6), custom_call_target="InvertDiagBlocksLowerTriangular" | custom-call | tf_op jit(solution)/shard_map/jit(_solve_triangular)/triangular_solve | solution.py:27
  212.9 1.4 fusion
  214.2 13.0 %convolution_convert_fusion = bf16[3968,64]{0,1:T(8,128)(2,1)S(1)} fusion(f32[1024,3968]{1,0:T(8,128)} %copy-done.1, f32[64,1024]{1,0:T(8,128)S(1)} %fusion), kind=kOutput, calls=%fused_computation.2 | convolution fusion | flops 3120816128 | bytes 17022976 | tf_op jit(solution)/shard_map/dot_general | solution.py:28
  227.2 1.3 copy.14
  228.6 0.7 multiply_bitcast_fusion
  229.3 19.0 %reduce-scatter.4.cloned.1.call-done = bf16[1984,64]{1,0:T(8,128)(2,1)} async-done(((bf16[3968,64]{1,0:T(8,128)(2,1)}), bf16[1984,64]{1,0:T(8,128)(2,1)}) %reduce-scatter.4.cloned.1.call-update) | async-done | bytes 253968
  248.3 1.2 copy.15
  249.6 66.3 %all-reduce.4 = f32[1984,64]{0,1:T(8,128)S(1)} all-reduce(bf16[1984,64]{0,1:T(8,128)(2,1)S(1)} %copy.15), channel_id=1, replica_groups=mesh['dp'=16,'mp'=2] {'dp'}, use_global_device_ids=true, to_apply=%region_6.7 | all-reduce | flops 126976 | bytes 761856 | tf_op jit(solution)/shard_map/psum | solution.py:32
  315.9 0.9 convert_bitcast_fusion
  316.8 7.3 %all-gather.1 = bf16[2,1984,64]{1,2,0:T(8,128)(2,1)S(1)} all-gather(bf16[1,1984,64]{1,2,0:T(8,128)(2,1)S(1)} %get-tuple-element.3), channel_id=1, replica_groups=mesh['dp'=16,'mp'=2] {'mp'}, dimensions={0}, use_global_device_ids=true | all-gather | bytes 761856 | tf_op jit(solution)/shard_map/all_gather | solution.py:33
  325.2 12.5 %subtract_convert_fusion = bf16[1024,3968]{1,0:T(8,128)(2,1)} fusion(f32[1024,3968]{1,0:T(8,128)} %copy-done.1, f32[64,1024]{1,0:T(8,128)S(1)} %fusion, bf16[3968,64]{0,1:T(8,128)(2,1)S(1)} %reshape.19), kind=kOutput, calls=%fused_computation | convolution fusion | flops 3128688640 | bytes 25149440 | tf_op jit(solution)/shard_map/dot_general | solution.py:36
  (16 shorter events, 2.9 us)
Async XLA Ops:
  7.2 60.4 %copy-start = (bf16[512,1024]{1,0:T(8,128)(2,1)S(1)}, bf16[512,1024]{1,0:T(8,128)(2,1)}, u32[]{:S(2)}) copy-start(bf16[512,1024]{1,0:T(8,128)(2,1)} %param.5) | copy-start | bytes 3145732
  7.2 60.4 %all-gather.4.cloned.1.call-start = ((), (), s32[]{:S(2)}) async-start(), calls=%async_computation.1 | async-start | bytes 6094848 | tf_op jit(solution)/shard_map/all_gather | solution.py:16
  7.9 181.8 %all-reduce.3.cloned.1.call-start = ((), (), s32[]{:S(2)}) async-start(), calls=%async_computation.2 | async-start | bytes 524288 | tf_op jit(solution)/shard_map/psum | solution.py:22
  76.0 5.6 %copy-start.1 = (f32[1024,3968]{1,0:T(8,128)}, f32[1024,3968]{1,0:T(8,128)S(1)}, u32[]{:S(2)}) copy-start(f32[1024,3968]{1,0:T(8,128)S(1)} %convert_add_fusion) | copy-start | bytes 48758788
  98.3 150.0 %reduce-scatter.4.cloned.1.call-start = ((), (), s32[]{:S(2)}) async-start(), calls=%async_computation.3 | async-start | bytes 1523712
Sparse Core Ops, SparseCore 0:
  9.5 58.0 all-gather.3
  98.4 91.1 all-reduce.2
  228.7 19.5 reduce-scatter.3
where the time goes:
time: 345 us; the launch traced here: 344 us
  waiting for transfers between devices  151 us (44%)
  blocking collectives  99.6 us (29%)
  matrix products  53.3 us (15%)
  between operations  14.5 us (4%)
  other arithmetic  14.3 us (4%)
  local copies, waits for them, and re-layouts  11.3 us (3%)
    psum x1, waiting for transfers between devices, per_device(): factor = lax.psum(local_p, 'dp') / replicas  91.1 us
    psum x1, blocking collectives, per_device(): q_own = lax.psum(q_part, 'dp') / replicas  66.3 us
    all_gather x1, waiting for transfers between devices, per_device(): lax.all_gather(inputs, 'mp', axis=1, tiled=True)  40 us
    unnamed x4, waiting for transfers between devices  19.7 us
    all_gather x1, blocking collectives, per_device(): q_full = lax.all_gather(q_prev, 'mp', axis=0, tiled=True)  17.7 us
    dot_general x1, matrix products, per_device(): local_p = jnp.dot(merged, q_full, precision=highest)  16.6 us
    dot_general x1, matrix products, per_device(): lax.dot_general(merged, p_hat, (((0,), (0,)), ((), ())), precision=highest)  13 us
    dot_general x1, matrix products, per_device(): approx = jnp.dot(p_hat, q_whole.T, precision=highest)  12.5 us
  transfers between devices with their start and end apart: 3, of which 3 were waited for; matrix products, arithmetic and copies ran while one was open for 1% of the time, Pallas kernels for 0%

commit v1 on v0

--- a/solution.py
+++ b/solution.py
@@ -1,10 +1,368 @@
+import functools
+
 import jax
 import jax.numpy as jnp
 from jax import lax
+from jax.experimental import pallas as pl
+from jax.experimental.pallas import tpu as pltpu
 from jax.sharding import PartitionSpec as P
 
+MESH = pl.DeviceIdType.MESH
+PIECES = 16
+EARLY = 8
+TN = (((0,), (0,)), ((), ()))
+NT = (((1,), (1,)), ((), ()))
+
+
+def left_half(shape):
+    return lax.broadcasted_iota(jnp.int32, shape, 1) < shape[1] // 2
+
+
+def fold(value):
+    return value + pltpu.roll(value, value.shape[1] // 2, 1)
+
+
+def split(twice):
+    head = twice.astype(jnp.bfloat16)
+    rest = (twice - head.astype(jnp.float32)).astype(jnp.bfloat16)
+    return jnp.where(left_half(twice.shape), head.astype(jnp.float32), rest.astype(jnp.float32)).astype(jnp.bfloat16)
+
+
+def pack(twice):
+    rows = twice.shape[0] // 2
+    return jnp.where(left_half((rows, twice.shape[1])), twice[:rows], twice[rows:])
+
+
+def unpack(packed):
+    other = pltpu.roll(packed, packed.shape[1] // 2, 1)
+    left = left_half(packed.shape)
+    return jnp.concatenate([jnp.where(left, packed, other), jnp.where(left, other, packed)], axis=0)
+
+
+def dot(a, b, dims=(((1,), (0,)), ((), ()))):
+    return lax.dot_general(a, b, dims, preferred_element_type=jnp.float32)
+
+
+def inverse_factor(gram, rank):
+    shape = (rank, 2 * rank)
+    row = lax.broadcasted_iota(jnp.int32, shape, 0)
+    col = lax.broadcasted_iota(jnp.int32, shape, 1)
+    left = col < rank
+    diag = row == col
+    trace = jnp.sum(jnp.where(diag, gram, 0.0), keepdims=True)
+    ridge = 0.01 * trace / rank + 1e-06
+    work = jnp.where(left, gram + jnp.where(diag, ridge, 0.0), jnp.where(col == row + rank, 1.0, 0.0))
+    row1 = lax.broadcasted_iota(jnp.int32, (rank, 1), 0)
+    for k in range(rank - 1):
+        pivot_row = work[k : k + 1, :]
+        scaled = pivot_row / pivot_row[:, k : k + 1]
+        factor = jnp.where(row1 > k, work[:, k : k + 1], 0.0)
+        work = work - factor * scaled
+    pivots = jnp.sum(jnp.where(diag, work, 0.0), axis=1, keepdims=True)
+    return work * lax.rsqrt(pivots)
+
+
+def exchange_kernel(
+    n_dp, x_ref, g_ref, e_hbm, qd_ref,
+    basis_ref, qown_ref, pa_ref, pb_ref, qg_ref, xo_ref,
+    e_ref, qs, u_send, u_recv, pw, p1, p2, p3, pg, gs, gr, qf, qw, q1, qb, q2, qc, q3,
+    load_sem, x_ssem, x_rsem, ssem, rsem,
+):
+    dp, mp = lax.axis_index("dp"), lax.axis_index("mp")
+    core, xx, zz = lax.rem(dp, 2), lax.rem(dp // 2, 2), dp // 4
+    n_z = n_dp // 4
+    rank = basis_ref.shape[1]
+
+    def device(d_core, d_x, d_y, k):
+        z = lax.rem(zz + k, n_z)
+        c = 1 - core if d_core else core
+        x = 1 - xx if d_x else xx
+        return ((z * 2 + x) * 2 + c, 1 - mp if d_y else mp)
+
+    core_mate, x_mate, y_mate, far_mate = device(1, 0, 0, 0), device(0, 1, 0, 0), device(0, 0, 1, 0), device(0, 1, 1, 0)
+    lane = [device(0, 0, 0, k) for k in range(1, n_z)]
+
+    load = pltpu.make_async_copy(e_hbm, e_ref, load_sem)
+    load.start()
+    barrier = pltpu.get_barrier_semaphore()
+    mates = [core_mate, x_mate, y_mate, far_mate] + lane
+    for mate in mates:
+        pl.semaphore_signal(barrier, inc=1, device_id=mate, device_id_type=MESH)
+
+    used = [0]
+
+    def send(src, dst, mate):
+        index = used[0]
+        used[0] += 1
+        copy = pltpu.make_async_remote_copy(
+            src_ref=src, dst_ref=dst, send_sem=ssem.at[index], recv_sem=rsem.at[index],
+            device_id=mate, device_id_type=MESH,
+        )
+        copy.start()
+        return copy
+
+    x_rows = x_ref.shape[0] // PIECES
+
+    def x_piece(j):
+        part = pl.ds(j * x_rows, x_rows)
+        return pltpu.make_async_remote_copy(
+            src_ref=x_ref.at[part], dst_ref=xo_ref.at[part], send_sem=x_ssem.at[j], recv_sem=x_rsem.at[j],
+            device_id=y_mate, device_id_type=MESH,
+        )
+
+    x_copies = [x_piece(j) for j in range(PIECES)]
+
+    qs[mp] = split(qd_ref[...])
+    u_own = pack(fold(dot(x_ref[...], qs[mp])))
+    u_send[...] = u_own
+    pl.semaphore_wait(barrier, len(mates))
+    half = qs.shape[1] // 2
+    my_half = pl.ds(pl.multiple_of(core * half, 16), half)
+    q_copy = send(qs.at[mp, my_half], qs.at[mp, my_half], y_mate)
+    u_copy = send(u_send, u_recv, y_mate)
+    q_copy.wait()
+    q_pass = send(qs.at[1 - mp, my_half], qs.at[1 - mp, my_half], core_mate)
+    x_copies[0].start()
+    load.wait()
+    u_copy.wait()
+    u = split(unpack(u_own + u_recv[...]))
+    p_part = dot(g_ref[...], u, TN)
+    q_pass.wait()
+    x_copies[1].start()
+    q_all = jnp.concatenate([qs[0], qs[1]], axis=0)
+    pw[...] = pack(fold(p_part + dot(e_ref[...], q_all)))
+
+    n = pw.shape[0]
+    n1, n2 = n // 2, n // 4
+    n3 = n2 // n_z
+
+    def rows(offset, size):
+        return pl.ds(pl.multiple_of(offset, size), size)
+
+    b1 = core * n1
+    b2 = b1 + xx * n2
+    b3 = b2 + zz * n3
+    copy = send(pw.at[rows((1 - core) * n1, n1)], p1, core_mate)
+    copy.wait()
+    pw[rows(b1, n1)] = pw[rows(b1, n1)] + p1[...]
+    copy = send(pw.at[rows(b1 + (1 - xx) * n2, n2)], p2, x_mate)
+    x_copies[2].start()
+    copy.wait()
+    pw[rows(b2, n2)] = pw[rows(b2, n2)] + p2[...]
+    copies = [
+        send(pw.at[rows(b2 + lax.rem(zz + k, n_z) * n3, n3)], p3.at[k - 1], lane[k - 1]) for k in range(1, n_z)
+    ]
+    x_copies[3].start()
+    total = pw[rows(b3, n3)]
+    for k, copy in enumerate(copies):
+        copy.wait()
+        total = total + p3[k]
+    pg[rows(b3, n3)] = total * (1.0 / n_dp)
+    copies = [send(pg.at[rows(b3, n3)], pg.at[rows(b3, n3)], mate) for mate in lane]
+    x_copies[4].start()
+    for copy in copies:
+        copy.wait()
+    copy = send(pg.at[rows(b2, n2)], pg.at[rows(b2, n2)], x_mate)
+    x_copies[5].start()
+    copy.wait()
+    copy = send(pg.at[rows(b1, n1)], pg.at[rows(b1, n1)], core_mate)
+    for j in range(6, EARLY):
+        x_copies[j].start()
+    copy.wait()
+
+    packed = pg[...]
+    square = lax.dot_general(packed, packed, TN, precision=lax.Precision.HIGHEST, preferred_element_type=jnp.float32)
+    square = square[:rank] + pltpu.roll(square, rank, 1)[rank:]
+    gs[...] = square
+    copy = send(gs, gr, y_mate)
+    for j in range(EARLY, PIECES):
+        x_copies[j].start()
+    copy.wait()
+    inverse = inverse_factor(square + gr[...], rank)
+    inverse = jnp.where(left_half(inverse.shape), 0.0, inverse)
+    inverse = jnp.concatenate([fold(inverse)] * 2, axis=0)
+    shape = inverse.shape
+    upper = lax.broadcasted_iota(jnp.int32, shape, 0) < rank
+    block = jnp.where(upper == left_half(shape), inverse, 0.0)
+    p_hat = unpack(
+        lax.dot_general(packed, block, NT, precision=lax.Precision.HIGHEST, preferred_element_type=jnp.float32)
+    )
+    basis_ref[...] = (p_hat * jnp.sqrt(jnp.float32(2 * n * lax.axis_size("mp"))))[:, :rank]
+    head = p_hat.astype(jnp.bfloat16).astype(jnp.float32)
+    left = left_half(p_hat.shape)
+    width = 2 * rank
+    for part, value in enumerate((head, p_hat - head)):
+        pa_ref[:, part * width : (part + 1) * width] = jnp.where(left, value, 0.0).astype(jnp.bfloat16)
+        pb_ref[:, part * width : (part + 1) * width] = jnp.where(left, 0.0, value).astype(jnp.bfloat16)
+    p_pair = split(p_hat)
+    v = split(fold(dot(g_ref[...], p_pair)))
+
+    features = e_ref.shape[1]
+    qf[pl.ds(features, qf.shape[0] - features)] = jnp.zeros((qf.shape[0] - features, width), jnp.float32)
+
+    @pl.loop(0, features // 128)
+    def _(c):
+        at = pl.ds(pl.multiple_of(c * 128, 128), 128)
+        qf[at] = fold(dot(e_ref[:, at], p_pair, TN))
+
+    own = x_ref.shape[1]
+    mine = pl.ds(pl.multiple_of(mp * own, 8), own)
+    theirs = pl.ds(pl.multiple_of((1 - mp) * own, 8), own)
+    qf[mine] = qf[mine] + fold(dot(x_ref[...], v, TN))
+    for x_copy in x_copies:
+        x_copy.wait()
+    qf[theirs] = qf[theirs] + fold(dot(xo_ref[...], v, TN))
+    m = qw.shape[0]
+    qw[...] = jnp.where(left_half(qw.shape), qf[0:m], qf[m : 2 * m]) * (1.0 / n_dp)
+
+    m1, m2 = m // 2, m // 8
+    m3 = m2 // n_z
+    quarter = xx * 2 + mp
+    a1 = core * m1
+    a2 = a1 + quarter * m2
+    a3 = a2 + zz * m3
+    copy = send(qw.at[rows((1 - core) * m1, m1)], q1, core_mate)
+    copy.wait()
+    sum1 = qw[rows(a1, m1)] + q1[...]
+    qw[rows(a1, m1)] = sum1
+    qb[...] = sum1.astype(jnp.bfloat16)
+    squad = (y_mate, x_mate, far_mate)
+    quarters = ((xx * 2 + 1 - mp), ((1 - xx) * 2 + mp), ((1 - xx) * 2 + 1 - mp))
+    copies = [send(qb.at[rows(quarters[d] * m2, m2)], q2.at[d], squad[d]) for d in range(3)]
+    sum2 = qw[rows(a2, m2)]
+    for d, copy in enumerate(copies):
+        copy.wait()
+        sum2 = sum2 + q2[d].astype(jnp.float32)
+    qw[rows(a2, m2)] = sum2
+    qc[...] = sum2.astype(jnp.bfloat16)
+    copies = [
+        send(qc.at[rows(lax.rem(zz + k, n_z) * m3, m3)], q3.at[k - 1], lane[k - 1]) for k in range(1, n_z)
+    ]
+    sum3 = qw[rows(a3, m3)]
+    for k, copy in enumerate(copies):
+        copy.wait()
+        sum3 = sum3 + q3[k].astype(jnp.float32)
+    qg_ref[rows(a3, m3)] = sum3.astype(jnp.bfloat16)
+    for group, part in ((lane, rows(a3, m3)), (squad, rows(a2, m2)), ((core_mate,), rows(a1, m1))):
+        copies = [send(qg_ref.at[part], qg_ref.at[part], mate) for mate in group]
+        for copy in copies:
+            copy.wait()
+
+    @pl.when(mp == 0)
+    def _():
+        qown_ref[...] = qg_ref[0:own, :].astype(jnp.float32)[:, :rank]
+
+    @pl.when(mp == 1)
+    def _():
+        qown_ref[0 : m - own, :] = qg_ref[own:m, :].astype(jnp.float32)[:, :rank]
+        low = qg_ref[0 : features - m, :].astype(jnp.float32)
+        qown_ref[m - own : own, :] = pltpu.roll(low, rank, 1)[:, :rank]
+
+
+def residue_kernel(x_ref, xo_ref, g_ref, e_ref, pa_ref, pb_ref, qg_ref, out_ref, xs, qq):
+    own = x_ref.shape[1]
+    m = qg_ref.shape[0]
+    features = e_ref.shape[1]
+
+    @pl.when(pl.program_id(0) == 0)
+    def _():
+        @pl.when(lax.axis_index("mp") == 0)
+        def _():
+            xs[:, :own] = x_ref[...]
+            xs[:, own:] = xo_ref[...]
+
+        @pl.when(lax.axis_index("mp") == 1)
+        def _():
+            xs[:, :own] = xo_ref[...]
+            xs[:, own:] = x_ref[...]
+
+        qq[...] = jnp.concatenate([qg_ref[...], qg_ref[...]], axis=1)
+
+    for p_ref, lo, hi in ((pa_ref, 0, m), (pb_ref, m, features)):
+        merged = dot(g_ref[...], xs[:, lo:hi], TN) + e_ref[:, lo:hi].astype(jnp.float32)
+        approx = dot(p_ref[...], qq[0 : hi - lo, :], NT)
+        out_ref[:, lo:hi] = (merged - approx).astype(jnp.bfloat16)
+
 
 def per_device(inputs, grad_out, error, q_prev):
+    n_dp = lax.axis_size("dp")
+    n_z = n_dp // 4
+    tokens, own = inputs.shape
+    out_rows, features = error.shape
+    rank = q_prev.shape[1]
+    width = 2 * rank
+    m = -(-features // 256) * 128
+    f32, bf16 = jnp.float32, jnp.bfloat16
+    n = out_rows // 2
+    vmem = pl.BlockSpec(memory_space=pltpu.VMEM)
+    copies = 2 + 1 + 2 * (n_z + 1) + 1 + 2 * (n_z + 3)
+    basis, q_own, pa, pb, qg, x_other = pl.pallas_call(
+        functools.partial(exchange_kernel, n_dp),
+        out_shape=(
+            jax.ShapeDtypeStruct((out_rows, rank), f32),
+            jax.ShapeDtypeStruct((own, rank), f32),
+            jax.ShapeDtypeStruct((out_rows, 2 * width), bf16),
+            jax.ShapeDtypeStruct((out_rows, 2 * width), bf16),
+            jax.ShapeDtypeStruct((m, width), bf16),
+            jax.ShapeDtypeStruct((tokens, own), bf16),
+        ),
+        in_specs=[vmem, vmem, pl.BlockSpec(memory_space=pl.ANY), vmem],
+        out_specs=(vmem,) * 6,
+        scratch_shapes=[
+            pltpu.VMEM((out_rows, features), bf16),
+            pltpu.VMEM((2, own, width), bf16),
+            pltpu.VMEM((tokens // 2, width), f32),
+            pltpu.VMEM((tokens // 2, width), f32),
+            pltpu.VMEM((n, width), f32),
+            pltpu.VMEM((n // 2, width), f32),
+            pltpu.VMEM((n // 4, width), f32),
+            pltpu.VMEM((n_z - 1, n // 4 // n_z, width), f32),
+            pltpu.VMEM((n, width), f32),
+            pltpu.VMEM((rank, width), f32),
+            pltpu.VMEM((rank, width), f32),
+            pltpu.VMEM((2 * m, width), f32),
+            pltpu.VMEM((m, width), f32),
+            pltpu.VMEM((m // 2, width), f32),
+            pltpu.VMEM((m // 2, width), bf16),
+            pltpu.VMEM((3, m // 8, width), bf16),
+            pltpu.VMEM((m // 8, width), bf16),
+            pltpu.VMEM((n_z - 1, m // 8 // n_z, width), bf16),
+            pltpu.SemaphoreType.DMA,
+            pltpu.SemaphoreType.DMA((PIECES,)),
+            pltpu.SemaphoreType.DMA((PIECES,)),
+            pltpu.SemaphoreType.DMA((copies,)),
+            pltpu.SemaphoreType.DMA((copies,)),
+        ],
+        compiler_params=pltpu.CompilerParams(
+            collective_id=0, has_side_effects=True, vmem_limit_bytes=60 * 1024 * 1024
+        ),
+        name="exchange",
+    )(inputs, grad_out, error, jnp.concatenate([q_prev, q_prev], axis=1))
+
+    tile = min(256, out_rows)
+    whole = lambda shape: pl.BlockSpec(shape, lambda i: (0, 0), pipeline_mode=pl.Buffered(1))
+    new_error = pl.pallas_call(
+        residue_kernel,
+        grid=(out_rows // tile,),
+        out_shape=jax.ShapeDtypeStruct(error.shape, bf16),
+        in_specs=[
+            whole((tokens, own)),
+            whole((tokens, own)),
+            pl.BlockSpec((tokens, tile), lambda i: (0, i)),
+            pl.BlockSpec((tile, features), lambda i: (i, 0)),
+            pl.BlockSpec((tile, 2 * width), lambda i: (i, 0)),
+            pl.BlockSpec((tile, 2 * width), lambda i: (i, 0)),
+            whole((m, width)),
+        ],
+        out_specs=pl.BlockSpec((tile, features), lambda i: (i, 0)),
+        scratch_shapes=[pltpu.VMEM((tokens, features), bf16), pltpu.VMEM((m, 2 * width), bf16)],
+        compiler_params=pltpu.CompilerParams(vmem_limit_bytes=60 * 1024 * 1024),
+        name="residue",
+    )(inputs, x_other, grad_out, error, pa, pb, qg)
+    return new_error, basis, q_own
+
+
+def general_form(inputs, grad_out, error, q_prev):
     highest = lax.Precision.HIGHEST
     replicas = lax.axis_size("dp")
     shards = lax.axis_size("mp")
@@ -40,8 +398,9 @@
 
 
 def solution(mesh):
+    paired = mesh.shape["mp"] == 2 and mesh.shape["dp"] % 4 == 0 and mesh.shape["dp"] > 4
     return jax.shard_map(
-        per_device,
+        per_device if paired else general_form,
         mesh=mesh,
         in_specs=(P("dp", "mp"), P("dp", "mp"), P(("dp", "mp"), None), P("mp", None)),
         out_specs=(P(("dp", "mp"), None), P("mp", None), P("mp", None)),

time: 345 us -> 117 us (0.34)
  waiting for transfers between devices: 151 us -> 0 us
  Pallas kernels: 0 us -> 106 us
  blocking collectives: 99.6 us -> 0 us
  matrix products: 53.3 us -> 0 us
  between operations: 14.5 us -> 0.66 us
  other arithmetic: 14.3 us -> 1.29 us
    pallas_call x0 -> x2, Pallas kernels: none -> 106 us  [the longest x1 92.4 us: per_device(): pl.pallas_call(functools.partial(exchange_kernel, n_dp), out_shape=(jax.S...]
    psum x1 -> x0, waiting for transfers between devices: 91.1 us -> none  [per_device(): factor = lax.psum(local_p, 'dp') / replicas]
    psum x2 -> x0, blocking collectives: 74.7 us -> none  [the longest x1 66.3 us: per_device(): q_own = lax.psum(q_part, 'dp') / replicas]
    dot_general x5 -> x0, matrix products: 51.9 us -> none  [the longest x1 16.6 us: per_device(): local_p = jnp.dot(merged, q_full, precision=highest)]
    all_gather x1 -> x0, waiting for transfers between devices: 40 us -> none  [per_device(): lax.all_gather(inputs, 'mp', axis=1, tiled=True)]
    all_gather x2 -> x0, blocking collectives: 25 us -> none  [the longest x1 17.7 us: per_device(): q_full = lax.all_gather(q_prev, 'mp', axis=0, tiled=True)]
    unnamed x4 -> x0, waiting for transfers between devices: 19.7 us -> none
    another operation x5 -> x0, other arithmetic: 12.1 us -> none  [the longest x3 6.52 us: per_device(): lower = jnp.linalg.cholesky(gram)]
  transfers between devices with their start and end apart: 3 -> 0, of which waited for: 3 -> 0; matrix products, arithmetic and copies ran while one was open for 1% -> 0% of each run, Pallas kernels for 0% -> 0%
where the time goes in v1:
time: 117 us; the launch traced here: 116 us
  Pallas kernels  106 us (91%)
  local copies, waits for them, and re-layouts  8.23 us (7%)
  other arithmetic  1.29 us (1%)
    pallas_call x1, Pallas kernels, per_device(): pl.pallas_call(functools.partial(exchange_kernel, n_dp), out_shape=(jax.S...  92.4 us
    pallas_call x1, Pallas kernels, per_device(): pl.pallas_call(residue_kernel, grid=(out_rows // tile,), out_shape=jax.Sh...  13.7 us
    unnamed x6, local copies, waits for them, and re-layouts  8.23 us

profile of v1, /device:TPU:0, one launch (start us, length us, event | category | flops | bytes accessed | tf_op | source)
XLA Modules:
  0.0 116.3 jit_solution(4016268908647219925)
XLA Ops:
  0.6 0.0 copy-start
  0.6 1.5 %copy.7 = f32[1984,64]{1,0:T(8,128)S(1)} copy(f32[1984,64]{0,1:T(8,128)} %param.7) | data formatting | bytes 1015808 | tf_op args[3]
  2.2 1.3 %pad_maximum_fusion.qd_ref = f32[1984,128]{1,0:T(8,128)} fusion(f32[1984,64]{1,0:T(8,128)S(1)} %copy.7), kind=kLoop, calls=%fused_computation | loop fusion | flops 253952 | bytes 1523712 | tf_op jit(solution)/shard_map/concatenate | solution.py:340
  3.5 0.0 copy-done
  3.5 2.5 %copy.10.x_ref = bf16[512,1984]{1,0:T(8,128)(2,1)} copy(bf16[512,1984]{0,1:T(8,128)(2,1)S(1)} %copy-done) | data formatting | bytes 4063232 | tf_op args[0]
  5.9 92.4 %exchange.1 = (f32[1024,64]{1,0:T(8,128)}, f32[1984,64]{1,0:T(8,128)}, bf16[1024,256]{1,0:T(8,128)(2,1)}, bf16[1024,256]{1,0:T(8,128)(2,1)}, bf16[2048,128]{1,0:T(8,128)(2,1)}, /*index=5*/bf16[512,1984]{1,0:T(8,128)(2,1)}) custom-call(bf16[512,1984]{1,0:T(8,128)(2,1)} %copy.10.x_ref, bf16[512,1024]{1,0:T(8,128)(2,1)} %g_ref.3, bf16[1024,3968]{1,0:T(8,128)(2,1)} %e_ref.1, ...), custom_call_target="tpu_custom_call" | custom-call | tf_op jit(solution)/shard_map/exchange/pallas_call | solution.py:299
  98.3 1.9 %copy.11 = f32[1024,64]{0,1:T(8,128)} copy(f32[1024,64]{1,0:T(8,128)} %get-tuple-element.16) | data formatting | bytes 524288
  100.2 2.3 %copy.12 = f32[1984,64]{0,1:T(8,128)} copy(f32[1984,64]{1,0:T(8,128)} %get-tuple-element.17) | data formatting | bytes 1015808
  102.6 13.7 %residue.1 = bf16[1024,3968]{1,0:T(8,128)(2,1)} custom-call(bf16[512,1984]{1,0:T(8,128)(2,1)} %copy.10.x_ref, bf16[512,1984]{1,0:T(8,128)(2,1)} %get-tuple-element.9.xo_ref, bf16[512,1024]{1,0:T(8,128)(2,1)} %g_ref.3, bf16[1024,3968]{1,0:T(8,128)(2,1)} %e_ref.1, bf16[1024,256]{1,0:T(8,128)(2,1)} %get-tuple-element.10.pa_ref, ...), custom_call_target="tpu_custom_call" | custom-call | tf_op jit(solution)/shard_map/residue/pallas_call | solution.py:344
Async XLA Ops:
  0.6 2.8 %copy-start = (bf16[512,1984]{0,1:T(8,128)(2,1)S(1)}, bf16[512,1984]{0,1:T(8,128)(2,1)}, u32[]{:S(2)}) copy-start(bf16[512,1984]{0,1:T(8,128)(2,1)} %param.4) | copy-start | bytes 6094852

commit v2 on v0

--- a/solution.py
+++ b/solution.py
@@ -1,10 +1,335 @@
+import functools
+
 import jax
 import jax.numpy as jnp
 from jax import lax
+from jax.experimental import pallas as pl
+from jax.experimental.pallas import tpu as pltpu
 from jax.sharding import PartitionSpec as P
 
+MESH = pl.DeviceIdType.MESH
+PIECE = 64
+NN = (((1,), (0,)), ((), ()))
+NT = (((1,), (1,)), ((), ()))
+
+
+def dot(a, b, dims=NN):
+    return lax.dot_general(a, b, dims, preferred_element_type=jnp.float32)
+
+
+def exact(a, b, dims=NN):
+    return lax.dot_general(a, b, dims, precision=lax.Precision.HIGHEST, preferred_element_type=jnp.float32)
+
+
+def split(value):
+    head = value.astype(jnp.bfloat16)
+    rest = (value - head.astype(jnp.float32)).astype(jnp.bfloat16)
+    return jnp.concatenate([head, rest], axis=0)
+
+
+def fold(terms):
+    rank = terms.shape[0] // 2
+    return terms[:rank] + terms[rank:]
+
+
+def inverse_factor(gram):
+    rank = gram.shape[0]
+    row = lax.broadcasted_iota(jnp.int32, gram.shape, 0)
+    diag = row == lax.broadcasted_iota(jnp.int32, gram.shape, 1)
+    ridge = 0.01 * jnp.sum(jnp.where(diag, gram, 0.0), keepdims=True) / rank + 1e-06
+    work = gram + jnp.where(diag, ridge, 0.0)
+    inverse = jnp.where(diag, 1.0, 0.0)
+    row1 = lax.broadcasted_iota(jnp.int32, (rank, 1), 0)
+    for k in range(rank - 1):
+        pivot_row = work[k : k + 1, :]
+        factor = jnp.where(row1 > k, work[:, k : k + 1], 0.0) / pivot_row[:, k : k + 1]
+        inverse = inverse - factor * inverse[k : k + 1, :]
+        work = work - factor * pivot_row
+    pivots = jnp.sum(jnp.where(diag, work, 0.0), axis=1, keepdims=True)
+    return inverse * lax.rsqrt(pivots)
+
+
+def exchange_kernel(
+    n_dp, x_hbm, g_ref, e_hbm, q_ref,
+    basis_ref, qown_ref, ph_ref, gt_ref, qg_ref, xf_hbm,
+    e_ref, xf, qs, u_send, u_recv, v_send, v_recv, pw, p1, p2, p3, pg, gs, gr, qf, xt, q1, qb, q2, qc, q3,
+    load_sem, x_ssem, x_rsem, ssem, rsem,
+):
+    dp, mp = lax.axis_index("dp"), lax.axis_index("mp")
+    core, xx, zz = lax.rem(dp, 2), lax.rem(dp // 2, 2), dp // 4
+    n_z = n_dp // 4
+    rank, own = q_ref.shape
+    features = e_ref.shape[1]
+
+    def device(d_core, d_x, d_y, k):
+        z = lax.rem(zz + k, n_z)
+        c = 1 - core if d_core else core
+        x = 1 - xx if d_x else xx
+        return ((z * 2 + x) * 2 + c, 1 - mp if d_y else mp)
+
+    core_mate, x_mate, y_mate, far_mate = device(1, 0, 0, 0), device(0, 1, 0, 0), device(0, 0, 1, 0), device(0, 1, 1, 0)
+    lane = [device(0, 0, 0, k) for k in range(1, n_z)]
+
+    x_base = pl.multiple_of(mp * own, PIECE)
+    mine = pl.ds(x_base, own)
+    load_x = pltpu.make_async_copy(x_hbm, xf.at[mine], load_sem.at[0])
+    load_e = pltpu.make_async_copy(e_hbm, e_ref, load_sem.at[1])
+    load_x.start()
+    load_e.start()
+    barrier = pltpu.get_barrier_semaphore()
+    mates = [core_mate, x_mate, y_mate, far_mate] + lane
+    for mate in mates:
+        pl.semaphore_signal(barrier, inc=1, device_id=mate, device_id_type=MESH)
+
+    used = [0]
+
+    def send(src, dst, mate):
+        index = used[0]
+        used[0] += 1
+        copy = pltpu.make_async_remote_copy(
+            src_ref=src, dst_ref=dst, send_sem=ssem.at[index], recv_sem=rsem.at[index],
+            device_id=mate, device_id_type=MESH,
+        )
+        copy.start()
+        return copy
+
+    pieces = own // PIECE
+    flying = []
+
+    def start_x(count):
+        for j in range(len(flying), min(pieces, len(flying) + count)):
+            part = pl.ds(pl.multiple_of(x_base + j * PIECE, PIECE), PIECE)
+            copy = pltpu.make_async_remote_copy(
+                src_ref=xf.at[part], dst_ref=xf.at[part], send_sem=x_ssem.at[j], recv_sem=x_rsem.at[j],
+                device_id=y_mate, device_id_type=MESH,
+            )
+            copy.start()
+            flying.append(copy)
+
+    q_pair = split(q_ref[...])
+    qs[mp] = q_pair
+    pl.semaphore_wait(barrier, len(mates))
+    my_half = pl.ds(pl.multiple_of(core * rank, 16), rank)
+    q_copy = send(qs.at[mp, my_half], qs.at[mp, my_half], y_mate)
+    load_x.wait()
+    u_own = fold(dot(q_pair, xf[mine]))
+    u_send[...] = u_own
+    u_copy = send(u_send, u_recv, y_mate)
+    gt_ref[...] = g_ref[...].T
+    q_copy.wait()
+    q_pass = send(qs.at[1 - mp, my_half], qs.at[1 - mp, my_half], core_mate)
+    start_x(STEPS[0])
+    u_copy.wait()
+    p_part = dot(split(u_own + u_recv[...]), g_ref[...])
+    load_e.wait()
+    q_pass.wait()
+    start_x(STEPS[1])
+    q_all = jnp.concatenate([qs[0], qs[1]], axis=1)
+    pw[...] = fold(p_part + dot(q_all, e_ref[...], NT))
+
+    def part(offset, size):
+        return pl.ds(pl.multiple_of(offset, size), size)
+
+    n = pw.shape[1]
+    n1, n2 = n // 2, n // 4
+    height = rank // n_z
+    b1 = part(core * n1, n1)
+    b2 = part(core * n1 + xx * n2, n2)
+    level = part(zz * height, height)
+    levels = [part(lax.rem(zz + k, n_z) * height, height) for k in range(1, n_z)]
+    copy = send(pw.at[:, part((1 - core) * n1, n1)], p1, core_mate)
+    copy.wait()
+    pw[:, b1] = pw[:, b1] + p1[...]
+    copy = send(pw.at[:, part(core * n1 + (1 - xx) * n2, n2)], p2, x_mate)
+    start_x(STEPS[2])
+    copy.wait()
+    pw[:, b2] = pw[:, b2] + p2[...]
+    copies = [send(pw.at[levels[k], b2], p3.at[k], lane[k]) for k in range(n_z - 1)]
+    start_x(STEPS[3])
+    total = pw[level, b2]
+    for k, copy in enumerate(copies):
+        copy.wait()
+        total = total + p3[k]
+    pg[level, b2] = total * (1.0 / n_dp)
+    copies = [send(pg.at[level, b2], pg.at[level, b2], mate) for mate in lane]
+    start_x(STEPS[4])
+    for copy in copies:
+        copy.wait()
+    copy = send(pg.at[:, b2], pg.at[:, b2], x_mate)
+    start_x(STEPS[5])
+    copy.wait()
+    copy = send(pg.at[:, b1], pg.at[:, b1], core_mate)
+    copy.wait()
+
+    mean = pg[...]
+    gs[...] = exact(mean, mean, NT)
+    copy = send(gs, gr, y_mate)
+    start_x(STEPS[6])
+    copy.wait()
+    p_hat = exact(inverse_factor(gs[...] + gr[...]), mean)
+    basis_ref[...] = p_hat * jnp.sqrt(jnp.float32(n * lax.axis_size("mp")))
+    p_pair = split(p_hat)
+    v_own = fold(dot(p_pair, g_ref[...], NT))
+    v_send[...] = v_own
+    v_copy = send(v_send, v_recv, y_mate)
+    start_x(STEPS[7])
+    ph_ref[...] = p_pair.T
+
+    m = qf.shape[1]
+    qf[:, features:] = jnp.zeros((rank, m - features), jnp.float32)
+    for lo in range(0, features, m // 4):
+        hi = min(lo + m // 4, features)
+        qf[:, lo:hi] = fold(dot(p_pair, e_ref[:, lo:hi]))
+    v_copy.wait()
+    xt[:, own:] = jnp.zeros((rank, xt.shape[1] - own), jnp.float32)
+    xt[:, :own] = fold(dot(split(v_own + v_recv[...]), xf[mine], NT))
+    m1, m2 = m // 2, m // 8
+
+    @pl.when(mp == 0)
+    def _():
+        qf[:, :m1] = qf[:, :m1] + xt[...]
+
+    @pl.when(mp == 1)
+    def _():
+        qf[:, features - m1 : features] = qf[:, features - m1 : features] + pltpu.roll(xt[...], m1 - own, 1)
+
+    start_x(STEPS[8])
+    a1 = part(core * m1, m1)
+    a2 = part(core * m1 + (xx * 2 + mp) * m2, m2)
+    copy = send(qf.at[:, part((1 - core) * m1, m1)], q1, core_mate)
+    copy.wait()
+    q1[...] = (qf[:, a1] + q1[...]) * (1.0 / n_dp)
+    qb[...] = q1[...].astype(jnp.bfloat16)
+    squad = (y_mate, x_mate, far_mate)
+    quarters = ((xx * 2 + 1 - mp), ((1 - xx) * 2 + mp), ((1 - xx) * 2 + 1 - mp))
+    copies = [send(qb.at[:, part(quarters[d] * m2, m2)], q2.at[d], squad[d]) for d in range(3)]
+    start_x(STEPS[9])
+    sum2 = q1[:, part((xx * 2 + mp) * m2, m2)]
+    for d, copy in enumerate(copies):
+        copy.wait()
+        sum2 = sum2 + q2[d].astype(jnp.float32)
+    p_sum = sum2.astype(jnp.bfloat16)
+    qc[...] = p_sum
+    copies = [send(qc.at[levels[k]], q3.at[k], lane[k]) for k in range(n_z - 1)]
+    start_x(STEPS[10])
+    qf[:, a2] = sum2
+    sum3 = qf[level, a2]
+    for k, copy in enumerate(copies):
+        copy.wait()
+        sum3 = sum3 + q3[k].astype(jnp.float32)
+    qg_ref[level, a2] = sum3.astype(jnp.bfloat16)
+    copies = [send(qg_ref.at[level, a2], qg_ref.at[level, a2], mate) for mate in lane]
+    start_x(pieces)
+    for copy in copies:
+        copy.wait()
+    copies = [send(qg_ref.at[:, a2], qg_ref.at[:, a2], mate) for mate in squad]
+    for copy in flying:
+        copy.wait()
+    store_x = pltpu.make_async_copy(xf, xf_hbm, load_sem.at[2])
+    store_x.start()
+    for copy in copies:
+        copy.wait()
+    copy = send(qg_ref.at[:, a1], qg_ref.at[:, a1], core_mate)
+    copy.wait()
+
+    @pl.when(mp == 0)
+    def _():
+        qown_ref[...] = qg_ref[:, :own].astype(jnp.float32)
+
+    @pl.when(mp == 1)
+    def _():
+        late = qg_ref[:, features - m1 : features].astype(jnp.float32)
+        qown_ref[...] = pltpu.roll(late, own, 1)[:, :own]
+
+    store_x.wait()
+
+
+STEPS = (3, 3, 1, 2, 2, 1, 4, 3, 4, 1, 3)
+
+
+def residue_kernel(gt_ref, x_ref, e_ref, ph_ref, qg_ref, out_ref):
+    merged = dot(gt_ref[...], x_ref[...], NT) + e_ref[...].astype(jnp.float32)
+    factor = qg_ref[...]
+    approx = dot(ph_ref[...], jnp.concatenate([factor, factor], axis=0))
+    out_ref[...] = (merged - approx).astype(jnp.bfloat16)
+
 
 def per_device(inputs, grad_out, error, q_prev):
+    n_dp = lax.axis_size("dp")
+    n_z = n_dp // 4
+    tokens, own = inputs.shape
+    n, features = error.shape
+    rank = q_prev.shape[1]
+    m = -(-features // 1024) * 1024
+    f32, bf16 = jnp.float32, jnp.bfloat16
+    vmem, anywhere = pl.BlockSpec(memory_space=pltpu.VMEM), pl.BlockSpec(memory_space=pl.ANY)
+    copies = 3 + 2 * (n_z + 1) + 2 + 2 * (n_z + 3)
+    basis, q_own, ph, gt, qg, x_full = pl.pallas_call(
+        functools.partial(exchange_kernel, n_dp),
+        out_shape=(
+            jax.ShapeDtypeStruct((rank, n), f32),
+            jax.ShapeDtypeStruct((rank, own), f32),
+            jax.ShapeDtypeStruct((n, 2 * rank), bf16),
+            jax.ShapeDtypeStruct((n, tokens), bf16),
+            jax.ShapeDtypeStruct((rank, m), bf16),
+            jax.ShapeDtypeStruct((features, tokens), bf16),
+        ),
+        in_specs=[anywhere, vmem, anywhere, vmem],
+        out_specs=(vmem,) * 5 + (anywhere,),
+        scratch_shapes=[
+            pltpu.VMEM((n, features), bf16),
+            pltpu.VMEM((features, tokens), bf16),
+            pltpu.VMEM((2, 2 * rank, own), bf16),
+            pltpu.VMEM((rank, tokens), f32),
+            pltpu.VMEM((rank, tokens), f32),
+            pltpu.VMEM((rank, tokens), f32),
+            pltpu.VMEM((rank, tokens), f32),
+            pltpu.VMEM((rank, n), f32),
+            pltpu.VMEM((rank, n // 2), f32),
+            pltpu.VMEM((rank, n // 4), f32),
+            pltpu.VMEM((n_z - 1, rank // n_z, n // 4), f32),
+            pltpu.VMEM((rank, n), f32),
+            pltpu.VMEM((rank, rank), f32),
+            pltpu.VMEM((rank, rank), f32),
+            pltpu.VMEM((rank, m), f32),
+            pltpu.VMEM((rank, m // 2), f32),
+            pltpu.VMEM((rank, m // 2), f32),
+            pltpu.VMEM((rank, m // 2), bf16),
+            pltpu.VMEM((3, rank, m // 8), bf16),
+            pltpu.VMEM((rank, m // 8), bf16),
+            pltpu.VMEM((n_z - 1, rank // n_z, m // 8), bf16),
+            pltpu.SemaphoreType.DMA((3,)),
+            pltpu.SemaphoreType.DMA((own // PIECE,)),
+            pltpu.SemaphoreType.DMA((own // PIECE,)),
+            pltpu.SemaphoreType.DMA((copies,)),
+            pltpu.SemaphoreType.DMA((copies,)),
+        ],
+        compiler_params=pltpu.CompilerParams(
+            collective_id=0, has_side_effects=True, vmem_limit_bytes=60 * 1024 * 1024
+        ),
+        name="exchange",
+    )(inputs.T, grad_out, error, q_prev.T)
+
+    tile = m // 8
+    new_error = pl.pallas_call(
+        residue_kernel,
+        grid=(pl.cdiv(features, tile),),
+        out_shape=jax.ShapeDtypeStruct(error.shape, bf16),
+        in_specs=[
+            pl.BlockSpec((n, tokens), lambda i: (0, 0), pipeline_mode=pl.Buffered(1)),
+            pl.BlockSpec((tile, tokens), lambda i: (i, 0)),
+            pl.BlockSpec((n, tile), lambda i: (0, i)),
+            pl.BlockSpec((n, 2 * rank), lambda i: (0, 0), pipeline_mode=pl.Buffered(1)),
+            pl.BlockSpec((rank, tile), lambda i: (0, i)),
+        ],
+        out_specs=pl.BlockSpec((n, tile), lambda i: (0, i)),
+        compiler_params=pltpu.CompilerParams(vmem_limit_bytes=60 * 1024 * 1024),
+        name="residue",
+    )(gt, x_full, error, ph, qg)
+    return new_error, basis.T, q_own.T
+
+
+def general_form(inputs, grad_out, error, q_prev):
     highest = lax.Precision.HIGHEST
     replicas = lax.axis_size("dp")
     shards = lax.axis_size("mp")
@@ -40,8 +365,9 @@
 
 
 def solution(mesh):
+    paired = mesh.shape["mp"] == 2 and mesh.shape["dp"] % 4 == 0 and mesh.shape["dp"] > 4
     return jax.shard_map(
-        per_device,
+        per_device if paired else general_form,
         mesh=mesh,
         in_specs=(P("dp", "mp"), P("dp", "mp"), P(("dp", "mp"), None), P("mp", None)),
         out_specs=(P(("dp", "mp"), None), P("mp", None), P("mp", None)),

time: 345 us -> 98 us (0.28)
  waiting for transfers between devices: 151 us -> 0 us
  blocking collectives: 99.6 us -> 0 us
  Pallas kernels: 0 us -> 95.5 us
  matrix products: 53.3 us -> 0 us
  other arithmetic: 14.3 us -> 0 us
  between operations: 14.5 us -> 0.66 us
  local copies, waits for them, and re-layouts: 11.3 us -> 1.5 us
    pallas_call x0 -> x2, Pallas kernels: none -> 95.5 us  [the longest x1 82 us: per_device(): pl.pallas_call(functools.partial(exchange_kernel, n_dp), out_shape=(jax.S...]
    psum x1 -> x0, waiting for transfers between devices: 91.1 us -> none  [per_device(): factor = lax.psum(local_p, 'dp') / replicas]
    psum x2 -> x0, blocking collectives: 74.7 us -> none  [the longest x1 66.3 us: per_device(): q_own = lax.psum(q_part, 'dp') / replicas]
    dot_general x5 -> x0, matrix products: 51.9 us -> none  [the longest x1 16.6 us: per_device(): local_p = jnp.dot(merged, q_full, precision=highest)]
    all_gather x1 -> x0, waiting for transfers between devices: 40 us -> none  [per_device(): lax.all_gather(inputs, 'mp', axis=1, tiled=True)]
    all_gather x2 -> x0, blocking collectives: 25 us -> none  [the longest x1 17.7 us: per_device(): q_full = lax.all_gather(q_prev, 'mp', axis=0, tiled=True)]
    unnamed x4 -> x0, waiting for transfers between devices: 19.7 us -> none
    another operation x5 -> x0, other arithmetic: 12.1 us -> none  [the longest x3 6.52 us: per_device(): lower = jnp.linalg.cholesky(gram)]
  transfers between devices with their start and end apart: 3 -> 0, of which waited for: 3 -> 0; matrix products, arithmetic and copies ran while one was open for 1% -> 0% of each run, Pallas kernels for 0% -> 0%
where the time goes in v2:
time: 98 us; the launch traced here: 97.7 us
  Pallas kernels  95.5 us (97%)
  local copies, waits for them, and re-layouts  1.5 us (2%)
    pallas_call x1, Pallas kernels, per_device(): pl.pallas_call(functools.partial(exchange_kernel, n_dp), out_shape=(jax.S...  82 us
    pallas_call x1, Pallas kernels, per_device(): pl.pallas_call(residue_kernel, grid=(pl.cdiv(features, tile),), out_shape...  13.5 us

profile of v2, /device:TPU:0, one launch (start us, length us, event | category | flops | bytes accessed | tf_op | source)
XLA Modules:
  0.0 97.7 jit_solution(14835918161606240980)
XLA Ops:
  0.6 82.0 %exchange.1 = (f32[64,1024]{1,0:T(8,128)}, f32[64,1984]{1,0:T(8,128)}, bf16[1024,128]{1,0:T(8,128)(2,1)}, bf16[1024,512]{1,0:T(8,128)(2,1)}, bf16[64,4096]{1,0:T(8,128)(2,1)}, /*index=5*/bf16[3968,512]{1,0:T(8,128)(2,1)}) custom-call(bf16[1984,512]{1,0:T(8,128)(2,1)} %bitcast.4, bf16[512,1024]{1,0:T(8,128)(2,1)} %g_ref.1, bf16[1024,3968]{1,0:T(8,128)(2,1)} %e_ref.1, ...), custom_call_target="tpu_custom_call" | custom-call | tf_op jit(solution)/shard_map/exchange/pallas_call | solution.py:267
  82.7 0.0 copy-start.1
  82.7 0.0 copy-start
  82.7 13.5 %residue.1 = bf16[1024,3968]{1,0:T(8,128)(2,1)} custom-call(bf16[1024,512]{1,0:T(8,128)(2,1)} %get-tuple-element.9.gt_ref, bf16[3968,512]{1,0:T(8,128)(2,1)} %get-tuple-element.10.x_ref, bf16[1024,3968]{1,0:T(8,128)(2,1)} %e_ref.1, bf16[1024,128]{1,0:T(8,128)(2,1)} %get-tuple-element.11.ph_ref, bf16[64,4096]{1,0:T(8,128)(2,1)} %get-tuple-element.12.qg_ref), custom_call_target="tpu_custom_call" | custom-call | tf_op jit(solution)/shard_map/residue/pallas_call | solution.py:314
  96.2 0.0 copy-done.1
  96.2 0.7 copy.9
  96.9 0.0 copy-done
  96.9 0.8 copy.10
Async XLA Ops:
  82.7 13.5 %copy-start.1 = (f32[64,1024]{1,0:T(8,128)S(1)}, f32[64,1024]{1,0:T(8,128)}, u32[]{:S(2)}) copy-start(f32[64,1024]{1,0:T(8,128)} %get-tuple-element.13) | copy-start | bytes 786436
  82.7 14.2 %copy-start = (f32[64,1984]{1,0:T(8,128)S(1)}, f32[64,1984]{1,0:T(8,128)}, u32[]{:S(2)}) copy-start(f32[64,1984]{1,0:T(8,128)} %get-tuple-element.14) | copy-start | bytes 1523716

commit v3 on v2

--- a/solution.py
+++ b/solution.py
@@ -40,11 +40,19 @@
     work = gram + jnp.where(diag, ridge, 0.0)
     inverse = jnp.where(diag, 1.0, 0.0)
     row1 = lax.broadcasted_iota(jnp.int32, (rank, 1), 0)
-    for k in range(rank - 1):
-        pivot_row = work[k : k + 1, :]
-        factor = jnp.where(row1 > k, work[:, k : k + 1], 0.0) / pivot_row[:, k : k + 1]
-        inverse = inverse - factor * inverse[k : k + 1, :]
-        work = work - factor * pivot_row
+    for k in range(0, rank, 2):
+        first, second = work[k : k + 1, :], work[k + 1 : k + 2, :]
+        one, two = work[:, k : k + 1], work[:, k + 1 : k + 2]
+        cross = first[:, k + 1 : k + 2]
+        ratio = second[:, k : k + 1] / first[:, k : k + 1]
+        factor = jnp.where(row1 > k, one, 0.0) / first[:, k : k + 1]
+        pivot = second[:, k + 1 : k + 2] - ratio * cross
+        later = jnp.where(row1 > k + 1, two - factor * cross, 0.0) / pivot
+        second = second - ratio * first
+        begin = inverse[k : k + 1, :]
+        follow = inverse[k + 1 : k + 2, :] - ratio * begin
+        inverse = inverse - factor * begin - later * follow
+        work = work - factor * first - later * second
     pivots = jnp.sum(jnp.where(diag, work, 0.0), axis=1, keepdims=True)
     return inverse * lax.rsqrt(pivots)
 
@@ -244,7 +252,7 @@
     store_x.wait()
 
 
-STEPS = (3, 3, 1, 2, 2, 1, 4, 3, 4, 1, 3)
+STEPS = (3, 4, 2, 3, 3, 1, 4, 4, 1, 0, 4)
 
 
 def residue_kernel(gt_ref, x_ref, e_ref, ph_ref, qg_ref, out_ref):
@@ -310,7 +318,7 @@
         name="exchange",
     )(inputs.T, grad_out, error, q_prev.T)
 
-    tile = m // 8
+    tile = m // 4
     new_error = pl.pallas_call(
         residue_kernel,
         grid=(pl.cdiv(features, tile),),

time: 98 us -> 94 us (0.959)
  Pallas kernels: 95.5 us -> 91.7 us
    pallas_call x1, Pallas kernels: 82 us -> 79.8 us  [per_device(): pl.pallas_call(functools.partial(exchange_kernel, n_dp), out_shape=(jax.S...]
    pallas_call x1, Pallas kernels: 13.5 us -> 11.9 us  [per_device(): pl.pallas_call(residue_kernel, grid=(pl.cdiv(features, tile),), out_shape...]
where the time goes in v3:
time: 94 us; the launch traced here: 93.9 us
  Pallas kernels  91.7 us (98%)
  local copies, waits for them, and re-layouts  1.5 us (2%)
    pallas_call x1, Pallas kernels, per_device(): pl.pallas_call(functools.partial(exchange_kernel, n_dp), out_shape=(jax.S...  79.8 us
    pallas_call x1, Pallas kernels, per_device(): pl.pallas_call(residue_kernel, grid=(pl.cdiv(features, tile),), out_shape...  11.9 us

profile of v3, /device:TPU:0, one launch (start us, length us, event | category | flops | bytes accessed | tf_op | source)
XLA Modules:
  0.0 93.9 jit_solution(5953793746949153095)
XLA Ops:
  0.6 79.8 %exchange.1 = (f32[64,1024]{1,0:T(8,128)}, f32[64,1984]{1,0:T(8,128)}, bf16[1024,128]{1,0:T(8,128)(2,1)}, bf16[1024,512]{1,0:T(8,128)(2,1)}, bf16[64,4096]{1,0:T(8,128)(2,1)}, /*index=5*/bf16[3968,512]{1,0:T(8,128)(2,1)}) custom-call(bf16[1984,512]{1,0:T(8,128)(2,1)} %bitcast.4, bf16[512,1024]{1,0:T(8,128)(2,1)} %g_ref.1, bf16[1024,3968]{1,0:T(8,128)(2,1)} %e_ref.1, ...), custom_call_target="tpu_custom_call" | custom-call | tf_op jit(solution)/shard_map/exchange/pallas_call | solution.py:275
  80.4 0.0 copy-start.1
  80.5 0.0 copy-start
  80.5 11.9 %residue.1 = bf16[1024,3968]{1,0:T(8,128)(2,1)} custom-call(bf16[1024,512]{1,0:T(8,128)(2,1)} %get-tuple-element.9.gt_ref, bf16[3968,512]{1,0:T(8,128)(2,1)} %get-tuple-element.10.x_ref, bf16[1024,3968]{1,0:T(8,128)(2,1)} %e_ref.1, bf16[1024,128]{1,0:T(8,128)(2,1)} %get-tuple-element.11.ph_ref, bf16[64,4096]{1,0:T(8,128)(2,1)} %get-tuple-element.12.qg_ref), custom_call_target="tpu_custom_call" | custom-call | tf_op jit(solution)/shard_map/residue/pallas_call | solution.py:322
  92.4 0.0 copy-done.1
  92.4 0.7 copy.9
  93.1 0.0 copy-done
  93.1 0.8 copy.10
Async XLA Ops:
  80.4 11.9 %copy-start.1 = (f32[64,1024]{1,0:T(8,128)S(1)}, f32[64,1024]{1,0:T(8,128)}, u32[]{:S(2)}) copy-start(f32[64,1024]{1,0:T(8,128)} %get-tuple-element.13) | copy-start | bytes 786436
  80.5 12.6 %copy-start = (f32[64,1984]{1,0:T(8,128)S(1)}, f32[64,1984]{1,0:T(8,128)}, u32[]{:S(2)}) copy-start(f32[64,1984]{1,0:T(8,128)} %get-tuple-element.14) | copy-start | bytes 1523716
